TPU v7x, 32 devices: a whole 2x2x4 slice. The times are simulated.
32 devices in a mesh: tm: 2 (over x), gx: 4 (over z), gy: 4 (over y, core).
Axes of the slice: x: 2, y: 2, z: 4, core: 2. Of those that a mesh axis runs over, the one named last changes fastest.
Arguments:
- initial: float32 [64, 16, 8, 128], P(None, 'gx', 'gy'), may hold values from -6 to 6
- source: float32 [64, 16, 8, 128], P(None, 'gx', 'gy'), may hold values from -1.5 to 1.5
- self_block: float32 [64, 64], replicated, may hold values from -1.01 to 0.01
- face_blocks: float32 [6, 64, 64], replicated, may hold values from -0.35 to 0.35
- coarse_block: float32 [64, 64], replicated, may hold values from -0.01 to 0.92
- face_code: int32 [16, 8, 128], P('gx', 'gy'), may hold values from 0 to 63
- step_counts: int32 [8], P('tm'), may hold values from 2 to 3, as said below
Outputs:
- final_states: float32 [8, 64, 16, 8, 128], P('tm', None, 'gx', 'gy')
Inputs may be any that keep to these rules, and one draw needn't show every extreme that they name: `step_counts`: some slice has exactly 3 steps in every draw.
All inputs are finite; a program needn't handle non-finite values.
Results may differ from a plain program's by a relative error of at most 0.0003.
Values sent between devices are 32-bit elements; how exact they have to be, the bound alone decides.
A program may use at most 128 MiB of HBM per device.

v0:
```python
import jax
import jax.numpy as jnp
from jax import lax
from jax.sharding import PartitionSpec as P

MAXSTEP = 3
ITERS = 2


HIGHEST = lax.Precision.HIGHEST


def with_halo(cells, sides, width):
    for axis, dim in sides:
        count = lax.axis_size(axis)
        head = lax.slice_in_dim(cells, 0, width, axis=dim)
        tail = lax.slice_in_dim(cells, cells.shape[dim] - width, cells.shape[dim], axis=dim)
        cells = jnp.concatenate(
            [
                lax.ppermute(tail, axis, [(i, (i + 1) % count) for i in range(count)]),
                cells,
                lax.ppermute(head, axis, [((i + 1) % count, i) for i in range(count)]),
            ],
            axis=dim,
        )
    return cells


def from_behind(value, axis, steps):
    count = lax.axis_size(axis)
    first, last = (max(0, -steps), min(count, count - steps))
    return lax.ppermute(value, axis, [(source, source + steps) for source in range(first, last)])


def blockwise(matrix, values):
    return jnp.einsum("ij,jxyz->ixyz", matrix, values, precision=HIGHEST)


def batched(matrix, values):
    return jnp.einsum("ij,sjxyz->sixyz", matrix, values, precision=HIGHEST)


def face_masks(face_code):
    powers = (2 ** jnp.arange(6)).astype(jnp.int32)
    return (face_code[None] // powers[:, None, None, None] % 2).astype(jnp.float32)


def coupled(padded, open_faces, self_block, face_blocks):
    center = padded[:, :, 1:-1, 1:-1]
    zero_plane = jnp.zeros_like(center[:, :, :, :, :1])
    below_plane = jnp.concatenate([zero_plane, center[:, :, :, :, :-1]], axis=4)
    above_plane = jnp.concatenate([center[:, :, :, :, 1:], zero_plane], axis=4)
    neighbours = [
        padded[:, :, :-2, 1:-1],
        padded[:, :, 2:, 1:-1],
        padded[:, :, 1:-1, :-2],
        padded[:, :, 1:-1, 2:],
        below_plane,
        above_plane,
    ]
    accumulated = batched(self_block, center)
    for facing in range(6):
        accumulated = accumulated + open_faces[facing] * batched(
            face_blocks[facing], neighbours[facing]
        )
    return accumulated


def per_device(initial, source, self_block, face_blocks, coarse_block, face_code, step_counts):
    slices_here = step_counts.shape[0]
    open_faces = face_masks(face_code)
    step_size = (1.0 / step_counts.astype(jnp.float32)).reshape(-1, 1, 1, 1, 1)
    step_limit = step_counts.reshape(-1, 1, 1, 1, 1)

    def section_rate(current):
        padded = with_halo(current, (("gx", 2), ("gy", 3)), 1)
        return coupled(padded, open_faces, self_block, face_blocks) + source

    def advance(number, current):
        slope_one = section_rate(current)
        middle = current + step_size * slope_one
        slope_two = section_rate(middle)
        moved = current + 0.5 * step_size * (slope_one + slope_two)
        return jnp.where(number < step_limit, moved, current)

    def run_local(incoming, corrections):
        starts = []
        finish_list = []
        current = incoming
        for position in range(slices_here):
            starts.append(current)
            current = blockwise(coarse_block, current) + corrections[position]
            finish_list.append(current)
        return (jnp.stack(starts), jnp.stack(finish_list), current)

    def sweep(corrections):
        time_devices = lax.axis_size("tm")
        position_tm = lax.axis_index("tm")

        def relay(number, incoming):
            unused_starts, unused_finish, leaving = run_local(incoming, corrections)
            arriving = from_behind(leaving, "tm", 1)
            return jnp.where(position_tm == 0, initial, arriving)

        incoming = lax.fori_loop(0, time_devices - 1, relay, initial)
        starts, finish_states, unused = run_local(incoming, corrections)
        return (starts, finish_states)

    corrections = jnp.broadcast_to(source, (slices_here,) + source.shape)
    starts, finish_states = sweep(corrections)
    for iteration in range(ITERS):
        finals = lax.fori_loop(0, MAXSTEP, advance, starts)
        corrections = finals - batched(coarse_block, starts)
        starts, finish_states = sweep(corrections)
    return finish_states


def solution(mesh):
    return jax.shard_map(
        per_device,
        mesh=mesh,
        in_specs=(
            P(None, "gx", "gy", None),
            P(None, "gx", "gy", None),
            P(),
            P(),
            P(),
            P("gx", "gy", None),
            P("tm"),
        ),
        out_specs=P("tm", None, "gx", "gy", None),
        check_vma=False,
    )
```

profile of v0, /device:TPU:0, one launch (start us, length us, event | category | flops | bytes accessed | tf_op | source)
XLA Modules:
  0.0 516.7 jit_solution(3195902168080084820)
XLA Ops:
  19.3 231.9 %while.16 = (s32[]{:T(128)}, f32[4,64,4,2,128]{4,1,3,2,0:T(8,128)S(1)}, s32[4,1,1,1,1]{0,4,3,2,1:T(1,128)S(1)}, f32[4,1,1,1,1]{0,4,3,2,1:T(1,128)S(1)}, f32[64,6...) while((s32[]{:T(128)}, ...), condition=%wide.region_1.2_spmd, body=%wide.region_0.1_spmd.sunk | while | flops 2833776640 | bytes 103745600 | solution.py:112
  38.9 14.3 %collective-permute-done.3 = f32[4,64,6,1,128]{4,1,3,2,0:T(8,128)} collective-permute-done((f32[4,64,6,1,128]{4,1,3,2,0:T(8,128)}, f32[4,64,6,1,128]{4,1,3,2,0:T(8,128)}, u32[]{:S(2)}, u32[]{:S(2)}) %collective-permute-start.3) | collective-permute-done | bytes 786464 | tf_op jit(solution)/shard_map/while/body/eval_jaxpr/ppermute | solution.py:20
  62.3 6.3 %collective-permute-done.4 = f32[4,64,1,2,128]{4,1,3,2,0:T(8,128)S(1)} collective-permute-done((f32[4,64,1,2,128]{4,1,3,2,0:T(8,128)S(1)}, f32[4,64,1,2,128]{4,1,3,2,0:T(8,128)S(1)}, u32[]{:S(2)}, u32[]{:S(2)}) %collective-permute-start.4) | collective-permute-done | bytes 262176 | tf_op jit(solution)/shard_map/while/body/eval_jaxpr/ppermute | solution.py:22
  68.6 6.0 %collective-permute-done.5 = f32[4,64,1,2,128]{4,1,3,2,0:T(8,128)S(1)} collective-permute-done((f32[4,64,1,2,128]{4,1,3,2,0:T(8,128)S(1)}, f32[4,64,1,2,128]{4,1,3,2,0:T(8,128)S(1)}, u32[]{:S(2)}, u32[]{:S(2)}) %collective-permute-start.5) | collective-permute-done | bytes 262176 | tf_op jit(solution)/shard_map/while/body/eval_jaxpr/ppermute | solution.py:20
  81.3 11.1 %collective-permute-done.7 = f32[4,64,6,1,128]{4,1,3,2,0:T(8,128)S(1)} collective-permute-done((f32[4,64,6,1,128]{4,1,3,2,0:T(8,128)S(1)}, f32[4,64,6,1,128]{4,1,3,2,0:T(8,128)S(1)}, u32[]{:S(2)}, u32[]{:S(2)}) %collective-permute-start.7) | collective-permute-done | bytes 786464 | tf_op jit(solution)/shard_map/while/body/eval_jaxpr/ppermute | solution.py:20
  117.7 15.1 %collective-permute-done.3 = f32[4,64,6,1,128]{4,1,3,2,0:T(8,128)} collective-permute-done((f32[4,64,6,1,128]{4,1,3,2,0:T(8,128)}, f32[4,64,6,1,128]{4,1,3,2,0:T(8,128)}, u32[]{:S(2)}, u32[]{:S(2)}) %collective-permute-start.3) | collective-permute-done | bytes 786464 | tf_op jit(solution)/shard_map/while/body/eval_jaxpr/ppermute | solution.py:20
  141.4 6.3 %collective-permute-done.4 = f32[4,64,1,2,128]{4,1,3,2,0:T(8,128)S(1)} collective-permute-done((f32[4,64,1,2,128]{4,1,3,2,0:T(8,128)S(1)}, f32[4,64,1,2,128]{4,1,3,2,0:T(8,128)S(1)}, u32[]{:S(2)}, u32[]{:S(2)}) %collective-permute-start.4) | collective-permute-done | bytes 262176 | tf_op jit(solution)/shard_map/while/body/eval_jaxpr/ppermute | solution.py:22
  158.8 10.9 %collective-permute-done.7 = f32[4,64,6,1,128]{4,1,3,2,0:T(8,128)S(1)} collective-permute-done((f32[4,64,6,1,128]{4,1,3,2,0:T(8,128)S(1)}, f32[4,64,6,1,128]{4,1,3,2,0:T(8,128)S(1)}, u32[]{:S(2)}, u32[]{:S(2)}) %collective-permute-start.7) | collective-permute-done | bytes 786464 | tf_op jit(solution)/shard_map/while/body/eval_jaxpr/ppermute | solution.py:20
  194.9 15.0 %collective-permute-done.3 = f32[4,64,6,1,128]{4,1,3,2,0:T(8,128)} collective-permute-done((f32[4,64,6,1,128]{4,1,3,2,0:T(8,128)}, f32[4,64,6,1,128]{4,1,3,2,0:T(8,128)}, u32[]{:S(2)}, u32[]{:S(2)}) %collective-permute-start.3) | collective-permute-done | bytes 786464 | tf_op jit(solution)/shard_map/while/body/eval_jaxpr/ppermute | solution.py:20
  218.5 6.1 %collective-permute-done.4 = f32[4,64,1,2,128]{4,1,3,2,0:T(8,128)S(1)} collective-permute-done((f32[4,64,1,2,128]{4,1,3,2,0:T(8,128)S(1)}, f32[4,64,1,2,128]{4,1,3,2,0:T(8,128)S(1)}, u32[]{:S(2)}, u32[]{:S(2)}) %collective-permute-start.4) | collective-permute-done | bytes 262176 | tf_op jit(solution)/shard_map/while/body/eval_jaxpr/ppermute | solution.py:22
  235.9 10.7 %collective-permute-done.7 = f32[4,64,6,1,128]{4,1,3,2,0:T(8,128)S(1)} collective-permute-done((f32[4,64,6,1,128]{4,1,3,2,0:T(8,128)S(1)}, f32[4,64,6,1,128]{4,1,3,2,0:T(8,128)S(1)}, u32[]{:S(2)}, u32[]{:S(2)}) %collective-permute-start.7) | collective-permute-done | bytes 786464 | tf_op jit(solution)/shard_map/while/body/eval_jaxpr/ppermute | solution.py:20
  259.1 6.5 %collective-permute-done.17 = f32[64,4,2,128]{3,0,2,1:T(8,128)S(1)} collective-permute-done((f32[64,4,2,128]{3,0,2,1:T(8,128)S(1)}, f32[64,4,2,128]{3,0,2,1:T(8,128)S(1)}, u32[]{:S(2)}, u32[]{:S(2)}) %collective-permute-start.17) | collective-permute-done | bytes 262176 | tf_op jit(solution)/shard_map/while/body/eval_jaxpr/ppermute | solution.py:32
  267.6 231.1 %while.17 = (s32[]{:T(128)}, f32[4,64,4,2,128]{4,1,3,2,0:T(8,128)S(1)}, s32[4,1,1,1,1]{0,4,3,2,1:T(1,128)S(1)}, f32[4,1,1,1,1]{0,4,3,2,1:T(1,128)S(1)}, f32[64,6...) while((s32[]{:T(128)}, ...), condition=%wide.region_3.4_spmd, body=%wide.region_2.3_spmd.sunk | while | flops 2833776640 | bytes 103745600 | solution.py:112
  287.9 14.8 %collective-permute-done.11 = f32[4,64,6,1,128]{4,1,3,2,0:T(8,128)} collective-permute-done((f32[4,64,6,1,128]{4,1,3,2,0:T(8,128)}, f32[4,64,6,1,128]{4,1,3,2,0:T(8,128)}, u32[]{:S(2)}, u32[]{:S(2)}) %collective-permute-start.11) | collective-permute-done | bytes 786464 | tf_op jit(solution)/shard_map/while/body/eval_jaxpr/ppermute | solution.py:20
  311.4 6.4 %collective-permute-done.12 = f32[4,64,1,2,128]{4,1,3,2,0:T(8,128)S(1)} collective-permute-done((f32[4,64,1,2,128]{4,1,3,2,0:T(8,128)S(1)}, f32[4,64,1,2,128]{4,1,3,2,0:T(8,128)S(1)}, u32[]{:S(2)}, u32[]{:S(2)}) %collective-permute-start.12) | collective-permute-done | bytes 262176 | tf_op jit(solution)/shard_map/while/body/eval_jaxpr/ppermute | solution.py:22
  317.8 5.2 %collective-permute-done.13 = f32[4,64,1,2,128]{4,1,3,2,0:T(8,128)S(1)} collective-permute-done((f32[4,64,1,2,128]{4,1,3,2,0:T(8,128)S(1)}, f32[4,64,1,2,128]{4,1,3,2,0:T(8,128)S(1)}, u32[]{:S(2)}, u32[]{:S(2)}) %collective-permute-start.13) | collective-permute-done | bytes 262176 | tf_op jit(solution)/shard_map/while/body/eval_jaxpr/ppermute | solution.py:20
  329.6 10.8 %collective-permute-done.15 = f32[4,64,6,1,128]{4,1,3,2,0:T(8,128)S(1)} collective-permute-done((f32[4,64,6,1,128]{4,1,3,2,0:T(8,128)S(1)}, f32[4,64,6,1,128]{4,1,3,2,0:T(8,128)S(1)}, u32[]{:S(2)}, u32[]{:S(2)}) %collective-permute-start.15) | collective-permute-done | bytes 786464 | tf_op jit(solution)/shard_map/while/body/eval_jaxpr/ppermute | solution.py:20
  365.6 15.0 %collective-permute-done.11 = f32[4,64,6,1,128]{4,1,3,2,0:T(8,128)} collective-permute-done((f32[4,64,6,1,128]{4,1,3,2,0:T(8,128)}, f32[4,64,6,1,128]{4,1,3,2,0:T(8,128)}, u32[]{:S(2)}, u32[]{:S(2)}) %collective-permute-start.11) | collective-permute-done | bytes 786464 | tf_op jit(solution)/shard_map/while/body/eval_jaxpr/ppermute | solution.py:20
  389.2 6.2 %collective-permute-done.12 = f32[4,64,1,2,128]{4,1,3,2,0:T(8,128)S(1)} collective-permute-done((f32[4,64,1,2,128]{4,1,3,2,0:T(8,128)S(1)}, f32[4,64,1,2,128]{4,1,3,2,0:T(8,128)S(1)}, u32[]{:S(2)}, u32[]{:S(2)}) %collective-permute-start.12) | collective-permute-done | bytes 262176 | tf_op jit(solution)/shard_map/while/body/eval_jaxpr/ppermute | solution.py:22
  406.7 10.7 %collective-permute-done.15 = f32[4,64,6,1,128]{4,1,3,2,0:T(8,128)S(1)} collective-permute-done((f32[4,64,6,1,128]{4,1,3,2,0:T(8,128)S(1)}, f32[4,64,6,1,128]{4,1,3,2,0:T(8,128)S(1)}, u32[]{:S(2)}, u32[]{:S(2)}) %collective-permute-start.15) | collective-permute-done | bytes 786464 | tf_op jit(solution)/shard_map/while/body/eval_jaxpr/ppermute | solution.py:20
  442.6 14.8 %collective-permute-done.11 = f32[4,64,6,1,128]{4,1,3,2,0:T(8,128)} collective-permute-done((f32[4,64,6,1,128]{4,1,3,2,0:T(8,128)}, f32[4,64,6,1,128]{4,1,3,2,0:T(8,128)}, u32[]{:S(2)}, u32[]{:S(2)}) %collective-permute-start.11) | collective-permute-done | bytes 786464 | tf_op jit(solution)/shard_map/while/body/eval_jaxpr/ppermute | solution.py:20
  466.1 6.4 %collective-permute-done.12 = f32[4,64,1,2,128]{4,1,3,2,0:T(8,128)S(1)} collective-permute-done((f32[4,64,1,2,128]{4,1,3,2,0:T(8,128)S(1)}, f32[4,64,1,2,128]{4,1,3,2,0:T(8,128)S(1)}, u32[]{:S(2)}, u32[]{:S(2)}) %collective-permute-start.12) | collective-permute-done | bytes 262176 | tf_op jit(solution)/shard_map/while/body/eval_jaxpr/ppermute | solution.py:22
  483.8 10.8 %collective-permute-done.15 = f32[4,64,6,1,128]{4,1,3,2,0:T(8,128)S(1)} collective-permute-done((f32[4,64,6,1,128]{4,1,3,2,0:T(8,128)S(1)}, f32[4,64,6,1,128]{4,1,3,2,0:T(8,128)S(1)}, u32[]{:S(2)}, u32[]{:S(2)}) %collective-permute-start.15) | collective-permute-done | bytes 786464 | tf_op jit(solution)/shard_map/while/body/eval_jaxpr/ppermute | solution.py:20
  506.7 6.4 %collective-permute-done.18 = f32[64,4,2,128]{3,0,2,1:T(8,128)S(1)} collective-permute-done((f32[64,4,2,128]{3,0,2,1:T(8,128)S(1)}, f32[64,4,2,128]{3,0,2,1:T(8,128)S(1)}, u32[]{:S(2)}, u32[]{:S(2)}) %collective-permute-start.18) | collective-permute-done | bytes 262176 | tf_op jit(solution)/shard_map/while/body/eval_jaxpr/ppermute | solution.py:32
  (365 shorter events, 297.9 us)
Async XLA Ops:
  35.0 18.3 %collective-permute-start.3 = (f32[4,64,6,1,128]{4,1,3,2,0:T(8,128)}, f32[4,64,6,1,128]{4,1,3,2,0:T(8,128)}, u32[]{:S(2)}, u32[]{:S(2)}) collective-permute-start(f32[4,64,6,1,128]{4,1,3,2,0:T(8,128)} %get-tuple-element.567), channel_id=1, source_target_pairs={{0,1},{1,2},{2,3},{3,0},{4,5},{5,6},{6,7},{7,4},{8,9},{9,10},{10,1... | collective-permute-start | bytes 2359304 | tf_op jit(solution)/shard_map/while/body/eval_jaxpr/ppermute | solution.py:20
  35.0 20.4 %collective-permute-start.2 = (f32[4,64,6,1,128]{4,1,3,2,0:T(8,128)}, f32[4,64,6,1,128]{4,1,3,2,0:T(8,128)}, u32[]{:S(2)}, u32[]{:S(2)}) collective-permute-start(f32[4,64,6,1,128]{4,1,3,2,0:T(8,128)} %get-tuple-element.565), channel_id=1, source_target_pairs={{1,0},{2,1},{3,2},{0,3},{5,4},{6,5},{7,6},{4,7},{9,8},{10,9},{11,1... | collective-permute-start | bytes 2359304 | tf_op jit(solution)/shard_map/while/body/eval_jaxpr/ppermute | solution.py:22
  74.9 17.5 %collective-permute-start.7 = (f32[4,64,6,1,128]{4,1,3,2,0:T(8,128)S(1)}, f32[4,64,6,1,128]{4,1,3,2,0:T(8,128)S(1)}, u32[]{:S(2)}, u32[]{:S(2)}) collective-permute-start(f32[4,64,6,1,128]{4,1,3,2,0:T(8,128)S(1)} %get-tuple-element.578), channel_id=1, source_target_pairs={{0,1},{1,2},{2,3},{3,0},{4,5},{5,6},{6,7},{7,4},{8,9},{9,10},{10,1... | collective-permute-start | bytes 2359304 | tf_op jit(solution)/shard_map/while/body/eval_jaxpr/ppermute | solution.py:20
  76.3 17.2 %collective-permute-start.6 = (f32[4,64,6,1,128]{4,1,3,2,0:T(8,128)S(1)}, f32[4,64,6,1,128]{4,1,3,2,0:T(8,128)S(1)}, u32[]{:S(2)}, u32[]{:S(2)}) collective-permute-start(f32[4,64,6,1,128]{4,1,3,2,0:T(8,128)S(1)} %get-tuple-element.577), channel_id=1, source_target_pairs={{1,0},{2,1},{3,2},{0,3},{5,4},{6,5},{7,6},{4,7},{9,8},{10,9},{11,1... | collective-permute-start | bytes 2359304 | tf_op jit(solution)/shard_map/while/body/eval_jaxpr/ppermute | solution.py:22
  113.7 19.0 %collective-permute-start.3 = (f32[4,64,6,1,128]{4,1,3,2,0:T(8,128)}, f32[4,64,6,1,128]{4,1,3,2,0:T(8,128)}, u32[]{:S(2)}, u32[]{:S(2)}) collective-permute-start(f32[4,64,6,1,128]{4,1,3,2,0:T(8,128)} %get-tuple-element.567), channel_id=1, source_target_pairs={{0,1},{1,2},{2,3},{3,0},{4,5},{5,6},{6,7},{7,4},{8,9},{9,10},{10,1... | collective-permute-start | bytes 2359304 | tf_op jit(solution)/shard_map/while/body/eval_jaxpr/ppermute | solution.py:20
  113.8 21.1 %collective-permute-start.2 = (f32[4,64,6,1,128]{4,1,3,2,0:T(8,128)}, f32[4,64,6,1,128]{4,1,3,2,0:T(8,128)}, u32[]{:S(2)}, u32[]{:S(2)}) collective-permute-start(f32[4,64,6,1,128]{4,1,3,2,0:T(8,128)} %get-tuple-element.565), channel_id=1, source_target_pairs={{1,0},{2,1},{3,2},{0,3},{5,4},{6,5},{7,6},{4,7},{9,8},{10,9},{11,1... | collective-permute-start | bytes 2359304 | tf_op jit(solution)/shard_map/while/body/eval_jaxpr/ppermute | solution.py:22
  152.3 17.3 %collective-permute-start.7 = (f32[4,64,6,1,128]{4,1,3,2,0:T(8,128)S(1)}, f32[4,64,6,1,128]{4,1,3,2,0:T(8,128)S(1)}, u32[]{:S(2)}, u32[]{:S(2)}) collective-permute-start(f32[4,64,6,1,128]{4,1,3,2,0:T(8,128)S(1)} %get-tuple-element.578), channel_id=1, source_target_pairs={{0,1},{1,2},{2,3},{3,0},{4,5},{5,6},{6,7},{7,4},{8,9},{9,10},{10,1... | collective-permute-start | bytes 2359304 | tf_op jit(solution)/shard_map/while/body/eval_jaxpr/ppermute | solution.py:20
  153.7 17.1 %collective-permute-start.6 = (f32[4,64,6,1,128]{4,1,3,2,0:T(8,128)S(1)}, f32[4,64,6,1,128]{4,1,3,2,0:T(8,128)S(1)}, u32[]{:S(2)}, u32[]{:S(2)}) collective-permute-start(f32[4,64,6,1,128]{4,1,3,2,0:T(8,128)S(1)} %get-tuple-element.577), channel_id=1, source_target_pairs={{1,0},{2,1},{3,2},{0,3},{5,4},{6,5},{7,6},{4,7},{9,8},{10,9},{11,1... | collective-permute-start | bytes 2359304 | tf_op jit(solution)/shard_map/while/body/eval_jaxpr/ppermute | solution.py:22
  190.9 18.9 %collective-permute-start.3 = (f32[4,64,6,1,128]{4,1,3,2,0:T(8,128)}, f32[4,64,6,1,128]{4,1,3,2,0:T(8,128)}, u32[]{:S(2)}, u32[]{:S(2)}) collective-permute-start(f32[4,64,6,1,128]{4,1,3,2,0:T(8,128)} %get-tuple-element.567), channel_id=1, source_target_pairs={{0,1},{1,2},{2,3},{3,0},{4,5},{5,6},{6,7},{7,4},{8,9},{9,10},{10,1... | collective-permute-start | bytes 2359304 | tf_op jit(solution)/shard_map/while/body/eval_jaxpr/ppermute | solution.py:20
  191.1 20.9 %collective-permute-start.2 = (f32[4,64,6,1,128]{4,1,3,2,0:T(8,128)}, f32[4,64,6,1,128]{4,1,3,2,0:T(8,128)}, u32[]{:S(2)}, u32[]{:S(2)}) collective-permute-start(f32[4,64,6,1,128]{4,1,3,2,0:T(8,128)} %get-tuple-element.565), channel_id=1, source_target_pairs={{1,0},{2,1},{3,2},{0,3},{5,4},{6,5},{7,6},{4,7},{9,8},{10,9},{11,1... | collective-permute-start | bytes 2359304 | tf_op jit(solution)/shard_map/while/body/eval_jaxpr/ppermute | solution.py:22
  229.4 17.1 %collective-permute-start.7 = (f32[4,64,6,1,128]{4,1,3,2,0:T(8,128)S(1)}, f32[4,64,6,1,128]{4,1,3,2,0:T(8,128)S(1)}, u32[]{:S(2)}, u32[]{:S(2)}) collective-permute-start(f32[4,64,6,1,128]{4,1,3,2,0:T(8,128)S(1)} %get-tuple-element.578), channel_id=1, source_target_pairs={{0,1},{1,2},{2,3},{3,0},{4,5},{5,6},{6,7},{7,4},{8,9},{9,10},{10,1... | collective-permute-start | bytes 2359304 | tf_op jit(solution)/shard_map/while/body/eval_jaxpr/ppermute | solution.py:20
  230.8 17.2 %collective-permute-start.6 = (f32[4,64,6,1,128]{4,1,3,2,0:T(8,128)S(1)}, f32[4,64,6,1,128]{4,1,3,2,0:T(8,128)S(1)}, u32[]{:S(2)}, u32[]{:S(2)}) collective-permute-start(f32[4,64,6,1,128]{4,1,3,2,0:T(8,128)S(1)} %get-tuple-element.577), channel_id=1, source_target_pairs={{1,0},{2,1},{3,2},{0,3},{5,4},{6,5},{7,6},{4,7},{9,8},{10,9},{11,1... | collective-permute-start | bytes 2359304 | tf_op jit(solution)/shard_map/while/body/eval_jaxpr/ppermute | solution.py:22
  284.0 18.8 %collective-permute-start.11 = (f32[4,64,6,1,128]{4,1,3,2,0:T(8,128)}, f32[4,64,6,1,128]{4,1,3,2,0:T(8,128)}, u32[]{:S(2)}, u32[]{:S(2)}) collective-permute-start(f32[4,64,6,1,128]{4,1,3,2,0:T(8,128)} %get-tuple-element.595), channel_id=1, source_target_pairs={{0,1},{1,2},{2,3},{3,0},{4,5},{5,6},{6,7},{7,4},{8,9},{9,10},{10,1... | collective-permute-start | bytes 2359304 | tf_op jit(solution)/shard_map/while/body/eval_jaxpr/ppermute | solution.py:20
  284.0 20.9 %collective-permute-start.10 = (f32[4,64,6,1,128]{4,1,3,2,0:T(8,128)}, f32[4,64,6,1,128]{4,1,3,2,0:T(8,128)}, u32[]{:S(2)}, u32[]{:S(2)}) collective-permute-start(f32[4,64,6,1,128]{4,1,3,2,0:T(8,128)} %get-tuple-element.593), channel_id=1, source_target_pairs={{1,0},{2,1},{3,2},{0,3},{5,4},{6,5},{7,6},{4,7},{9,8},{10,9},{11,1... | collective-permute-start | bytes 2359304 | tf_op jit(solution)/shard_map/while/body/eval_jaxpr/ppermute | solution.py:22
  323.2 17.2 %collective-permute-start.15 = (f32[4,64,6,1,128]{4,1,3,2,0:T(8,128)S(1)}, f32[4,64,6,1,128]{4,1,3,2,0:T(8,128)S(1)}, u32[]{:S(2)}, u32[]{:S(2)}) collective-permute-start(f32[4,64,6,1,128]{4,1,3,2,0:T(8,128)S(1)} %get-tuple-element.606), channel_id=1, source_target_pairs={{0,1},{1,2},{2,3},{3,0},{4,5},{5,6},{6,7},{7,4},{8,9},{9,10},{10,1... | collective-permute-start | bytes 2359304 | tf_op jit(solution)/shard_map/while/body/eval_jaxpr/ppermute | solution.py:20
  324.5 17.1 %collective-permute-start.14 = (f32[4,64,6,1,128]{4,1,3,2,0:T(8,128)S(1)}, f32[4,64,6,1,128]{4,1,3,2,0:T(8,128)S(1)}, u32[]{:S(2)}, u32[]{:S(2)}) collective-permute-start(f32[4,64,6,1,128]{4,1,3,2,0:T(8,128)S(1)} %get-tuple-element.605), channel_id=1, source_target_pairs={{1,0},{2,1},{3,2},{0,3},{5,4},{6,5},{7,6},{4,7},{9,8},{10,9},{11,1... | collective-permute-start | bytes 2359304 | tf_op jit(solution)/shard_map/while/body/eval_jaxpr/ppermute | solution.py:22
  361.6 18.9 %collective-permute-start.11 = (f32[4,64,6,1,128]{4,1,3,2,0:T(8,128)}, f32[4,64,6,1,128]{4,1,3,2,0:T(8,128)}, u32[]{:S(2)}, u32[]{:S(2)}) collective-permute-start(f32[4,64,6,1,128]{4,1,3,2,0:T(8,128)} %get-tuple-element.595), channel_id=1, source_target_pairs={{0,1},{1,2},{2,3},{3,0},{4,5},{5,6},{6,7},{7,4},{8,9},{9,10},{10,1... | collective-permute-start | bytes 2359304 | tf_op jit(solution)/shard_map/while/body/eval_jaxpr/ppermute | solution.py:20
  361.8 20.9 %collective-permute-start.10 = (f32[4,64,6,1,128]{4,1,3,2,0:T(8,128)}, f32[4,64,6,1,128]{4,1,3,2,0:T(8,128)}, u32[]{:S(2)}, u32[]{:S(2)}) collective-permute-start(f32[4,64,6,1,128]{4,1,3,2,0:T(8,128)} %get-tuple-element.593), channel_id=1, source_target_pairs={{1,0},{2,1},{3,2},{0,3},{5,4},{6,5},{7,6},{4,7},{9,8},{10,9},{11,1... | collective-permute-start | bytes 2359304 | tf_op jit(solution)/shard_map/while/body/eval_jaxpr/ppermute | solution.py:22
  400.2 17.2 %collective-permute-start.15 = (f32[4,64,6,1,128]{4,1,3,2,0:T(8,128)S(1)}, f32[4,64,6,1,128]{4,1,3,2,0:T(8,128)S(1)}, u32[]{:S(2)}, u32[]{:S(2)}) collective-permute-start(f32[4,64,6,1,128]{4,1,3,2,0:T(8,128)S(1)} %get-tuple-element.606), channel_id=1, source_target_pairs={{0,1},{1,2},{2,3},{3,0},{4,5},{5,6},{6,7},{7,4},{8,9},{9,10},{10,1... | collective-permute-start | bytes 2359304 | tf_op jit(solution)/shard_map/while/body/eval_jaxpr/ppermute | solution.py:20
  401.6 17.1 %collective-permute-start.14 = (f32[4,64,6,1,128]{4,1,3,2,0:T(8,128)S(1)}, f32[4,64,6,1,128]{4,1,3,2,0:T(8,128)S(1)}, u32[]{:S(2)}, u32[]{:S(2)}) collective-permute-start(f32[4,64,6,1,128]{4,1,3,2,0:T(8,128)S(1)} %get-tuple-element.605), channel_id=1, source_target_pairs={{1,0},{2,1},{3,2},{0,3},{5,4},{6,5},{7,6},{4,7},{9,8},{10,9},{11,1... | collective-permute-start | bytes 2359304 | tf_op jit(solution)/shard_map/while/body/eval_jaxpr/ppermute | solution.py:22
  438.7 18.8 %collective-permute-start.11 = (f32[4,64,6,1,128]{4,1,3,2,0:T(8,128)}, f32[4,64,6,1,128]{4,1,3,2,0:T(8,128)}, u32[]{:S(2)}, u32[]{:S(2)}) collective-permute-start(f32[4,64,6,1,128]{4,1,3,2,0:T(8,128)} %get-tuple-element.595), channel_id=1, source_target_pairs={{0,1},{1,2},{2,3},{3,0},{4,5},{5,6},{6,7},{7,4},{8,9},{9,10},{10,1... | collective-permute-start | bytes 2359304 | tf_op jit(solution)/shard_map/while/body/eval_jaxpr/ppermute | solution.py:20
  438.8 20.8 %collective-permute-start.10 = (f32[4,64,6,1,128]{4,1,3,2,0:T(8,128)}, f32[4,64,6,1,128]{4,1,3,2,0:T(8,128)}, u32[]{:S(2)}, u32[]{:S(2)}) collective-permute-start(f32[4,64,6,1,128]{4,1,3,2,0:T(8,128)} %get-tuple-element.593), channel_id=1, source_target_pairs={{1,0},{2,1},{3,2},{0,3},{5,4},{6,5},{7,6},{4,7},{9,8},{10,9},{11,1... | collective-permute-start | bytes 2359304 | tf_op jit(solution)/shard_map/while/body/eval_jaxpr/ppermute | solution.py:22
  477.3 17.2 %collective-permute-start.15 = (f32[4,64,6,1,128]{4,1,3,2,0:T(8,128)S(1)}, f32[4,64,6,1,128]{4,1,3,2,0:T(8,128)S(1)}, u32[]{:S(2)}, u32[]{:S(2)}) collective-permute-start(f32[4,64,6,1,128]{4,1,3,2,0:T(8,128)S(1)} %get-tuple-element.606), channel_id=1, source_target_pairs={{0,1},{1,2},{2,3},{3,0},{4,5},{5,6},{6,7},{7,4},{8,9},{9,10},{10,1... | collective-permute-start | bytes 2359304 | tf_op jit(solution)/shard_map/while/body/eval_jaxpr/ppermute | solution.py:20
  478.6 17.0 %collective-permute-start.14 = (f32[4,64,6,1,128]{4,1,3,2,0:T(8,128)S(1)}, f32[4,64,6,1,128]{4,1,3,2,0:T(8,128)S(1)}, u32[]{:S(2)}, u32[]{:S(2)}) collective-permute-start(f32[4,64,6,1,128]{4,1,3,2,0:T(8,128)S(1)} %get-tuple-element.605), channel_id=1, source_target_pairs={{1,0},{2,1},{3,2},{0,3},{5,4},{6,5},{7,6},{4,7},{9,8},{10,9},{11,1... | collective-permute-start | bytes 2359304 | tf_op jit(solution)/shard_map/while/body/eval_jaxpr/ppermute | solution.py:22
  (71 other events, 423.0 us)
where the time goes:
time: 521 us; the launch traced here: 517 us
  waiting for transfers between devices  279 us (54%)
  matrix products  140 us (27%)
  starting transfers between devices  71.5 us (14%)
  local copies, waits for them, and re-layouts  18.9 us (4%)
    ppermute x24, waiting for transfers between devices, with_halo(): lax.ppermute(tail, axis, [(i, (i + 1) % count) for i in range(count)])  198 us
    dot_general x86, matrix products, batched(): return jnp.einsum('ij,sjxyz->sixyz', matrix, values, precision=HIGHEST)  131 us
    ppermute x24, waiting for transfers between devices, with_halo(): lax.ppermute(head, axis, [((i + 1) % count, i) for i in range(count)])  64.5 us
    ppermute x24, starting transfers between devices, with_halo(): lax.ppermute(head, axis, [((i + 1) % count, i) for i in range(count)])  47.1 us
    ppermute x3, waiting for transfers between devices, from_behind(): lax.ppermute(value, axis, [(source, source + steps) for source in range(f...  17.1 us
    ppermute x3, starting transfers between devices, from_behind(): lax.ppermute(value, axis, [(source, source + steps) for source in range(f...  13.8 us
    ppermute x24, starting transfers between devices, with_halo(): lax.ppermute(tail, axis, [(i, (i + 1) % count) for i in range(count)])  10.6 us
  transfers between devices with their start and end apart: 51, of which 42 were waited for; matrix products, arithmetic and copies ran while one was open for 18% of the time, Pallas kernels for 0%

commit v1 on v0

v1 whole, which is shorter than its diff:
```python
import functools

import jax
import jax.numpy as jnp
from jax import lax
from jax.experimental import pallas as pl
from jax.experimental.pallas import tpu as pltpu
from jax.sharding import PartitionSpec as P

MAXSTEP = 3
ITERS = 2
MESH = pl.DeviceIdType.MESH


def split3(v):
    high = v.astype(jnp.bfloat16)
    low = (v - high.astype(jnp.float32)).astype(jnp.bfloat16)
    return jnp.concatenate([high, low, high], axis=0)


def split3_weights(w):
    high = w.astype(jnp.bfloat16)
    low = (w - high.astype(jnp.float32)).astype(jnp.bfloat16)
    return jnp.concatenate([high, high, low], axis=1)


def mul(w, v3):
    return jnp.dot(w, v3, preferred_element_type=jnp.float32)


def kernel(nt, nx, ny, mine, weights, step_ref, gain_ref, out,
           field, wide, prod, cur, mid, slope, corr, recv, local, starts, halo, arrived, powers, mixer,
           gsend, grecv, hsend, hrecv, asend, arecv, bsend, brecv, tsend, trecv):
    tm, gx, gy = lax.axis_index("tm"), lax.axis_index("gx"), lax.axis_index("gy")
    right, left = lax.rem(gx + 1, nx), lax.rem(gx + nx - 1, nx)
    later, earlier = lax.rem(tm + 1, nt), lax.rem(tm + nt - 1, nt)
    peers = [lax.rem(gy + d, ny) for d in range(1, ny)]
    xs = mine.shape[0]
    dof = weights.shape[1]

    barrier = pltpu.get_barrier_semaphore()
    for target in [{"gx": left}, {"gx": right}, {"tm": later}, {"tm": earlier}] + [{"gy": p} for p in peers]:
        pl.semaphore_signal(barrier, inc=1, device_id=target, device_id_type=MESH)
    pl.semaphore_wait(barrier, 4 + len(peers))

    def exchange(source_of, target, send, receive):
        copies = []
        for d, peer in enumerate(peers):
            copy = pltpu.make_async_remote_copy(
                src_ref=source_of(peer), dst_ref=target, send_sem=send.at[d], recv_sem=receive.at[d],
                device_id={"gy": peer}, device_id_type=MESH)
            copy.start()
            copies.append(copy)
        return copies

    copies = exchange(lambda peer: mine, field.at[:, gy], gsend, grecv)

    wide[...] = split3_weights(weights[...])
    coarse = wide[7 * dof:8 * dof, :]
    power = weights[7 * dof:8 * dof, :]
    for j in range(ny):
        powers[j * dof:(j + 1) * dof, :] = split3_weights(power)
        power = mul(coarse, split3(power)) if j < ny - 1 else power
    rows = lax.broadcasted_iota(jnp.int32, (dof, dof), 0)
    cols = lax.broadcasted_iota(jnp.int32, (dof, dof), 1)
    identity = (rows == cols).astype(jnp.float32)

    def raise_power(_, pair):
        high, total = pair
        return mul(coarse, split3(high)), mul(coarse, split3(total)) + identity

    high, total = lax.fori_loop(0, tm * ny + gy, raise_power, (identity, jnp.zeros_like(identity)))
    mixer[...] = jnp.concatenate([split3_weights(high), split3_weights(total)], axis=1)
    for x in range(xs):
        field[x, gy] = mine[x]
    for copy in copies:
        copy.wait()

    def first_starts(x, _):
        for y in range(ny):
            cur[x, y] = mul(mixer[...], jnp.concatenate(
                [split3(field[x, y, 0:dof, :]), split3(field[x, y, dof:2 * dof, :])], axis=0))
        return 0

    lax.fori_loop(0, xs, first_starts, 0)

    step = step_ref[gy]

    def combine(x, y):
        here = prod.at[x + 1, y]

        def mask(f):
            return field[x, y, 2 * dof + f:2 * dof + f + 1, :]

        lower, upper = prod.at[x + 1, (y + ny - 1) % ny], prod.at[x + 1, (y + 1) % ny]

        def face(f):
            return slice((f + 1) * dof, (f + 2) * dof)

        before = jnp.concatenate([lower[face(2), 128:], here[face(2), :128]], axis=1)
        after = jnp.concatenate([here[face(3), 128:], upper[face(3), :128]], axis=1)
        below = jnp.concatenate([pltpu.roll(here[face(4), :128], 1, 1), pltpu.roll(here[face(4), 128:], 1, 1)], axis=1)
        above = jnp.concatenate([pltpu.roll(here[face(5), :128], 127, 1), pltpu.roll(here[face(5), 128:], 127, 1)], axis=1)
        total = here[0:dof, :] + field[x, y, dof:2 * dof, :]
        total = total + mask(0) * prod[x, y, face(0), :]
        total = total + mask(1) * prod[x + 2, y, face(1), :]
        total = total + mask(2) * before
        total = total + mask(3) * after
        total = total + mask(4) * below
        return total + mask(5) * above

    def stage(second, finish):
        source = mid if second else cur
        slot = 1 if second else 0
        to_left = pltpu.make_async_remote_copy(
            src_ref=source.at[0], dst_ref=halo.at[slot, 1], send_sem=hsend.at[slot, 0], recv_sem=hrecv.at[slot, 1],
            device_id={"gx": left}, device_id_type=MESH)
        to_right = pltpu.make_async_remote_copy(
            src_ref=source.at[xs - 1], dst_ref=halo.at[slot, 0], send_sem=hsend.at[slot, 1], recv_sem=hrecv.at[slot, 0],
            device_id={"gx": right}, device_id_type=MESH)
        to_left.start()
        to_right.start()

        def products(x, _):
            for y in range(ny):
                prod[x + 1, y] = mul(wide[...], split3(source[x, y]))
            return 0

        lax.fori_loop(0, xs, products, 0)

        def inner(x, _):
            for y in range(ny):
                finish(x, y, combine(x, y))
            return 0

        lax.fori_loop(1, xs - 1, inner, 0)
        to_left.wait()
        to_right.wait()
        for y in range(ny):
            prod[0, y, dof:2 * dof, :] = mul(wide[dof:2 * dof, :], split3(halo[slot, 0, y]))
            prod[xs + 1, y, 2 * dof:3 * dof, :] = mul(wide[2 * dof:3 * dof, :], split3(halo[slot, 1, y]))
        for x in (0, xs - 1):
            for y in range(ny):
                finish(x, y, combine(x, y))

    def advance(number, _):
        gain = gain_ref[number, gy]

        def to_middle(x, y, rate):
            slope[x, y] = rate
            mid[x, y] = cur[x, y] + step * rate

        def to_next(x, y, rate):
            cur[x, y] = cur[x, y] + gain * (slope[x, y] + rate)

        stage(False, to_middle)
        stage(True, to_next)
        return 0

    for iteration in range(ITERS):
        def keep_coarse(x, _):
            for y in range(ny):
                corr[x, y] = mul(coarse, split3(cur[x, y]))
            return 0

        lax.fori_loop(0, xs, keep_coarse, 0)
        lax.fori_loop(0, MAXSTEP, advance, 0)

        def correct(x, _):
            for y in range(ny):
                corr[x, y] = cur[x, y] - corr[x, y]
            return 0

        lax.fori_loop(0, xs, correct, 0)
        copies = exchange(lambda peer: corr.at[:, peer], recv.at[gy], asend, arecv)
        for x in range(xs):
            recv[gy, x] = corr[x, gy]
        for copy in copies:
            copy.wait()

        def run_local(x, _):
            now = recv[0, x]
            local[0, x] = now
            for j in range(1, ny):
                now = mul(coarse, split3(now)) + recv[j, x]
                local[j, x] = now
            return 0

        lax.fori_loop(0, xs, run_local, 0)
        for x in range(xs):
            starts[0, x] = mine[x, 0:dof, :]
        for relay in range(nt - 1):
            at = iteration * (nt - 1) + relay
            for x in range(xs):
                starts[ny, x] = mul(powers[(ny - 1) * dof:, :], split3(starts[0, x])) + local[ny - 1, x]
            copy = pltpu.make_async_remote_copy(
                src_ref=starts.at[ny], dst_ref=arrived.at[at], send_sem=tsend.at[at], recv_sem=trecv.at[at],
                device_id={"tm": later}, device_id_type=MESH)
            copy.start()
            copy.wait()
            for x in range(xs):
                starts[0, x] = jnp.where(tm == 0, mine[x, 0:dof, :], arrived[at, x])
        last = iteration == ITERS - 1

        def finish_all(x, _):
            shares = mul(powers[...], split3(starts[0, x]))
            for j in range(ny):
                ended = shares[j * dof:(j + 1) * dof, :] + local[j, x]
                if last:
                    out[j, x] = ended
                elif j < ny - 1:
                    starts[j + 1, x] = ended
            return 0

        lax.fori_loop(0, xs, finish_all, 0)
        if not last:
            copies = exchange(lambda peer: starts.at[peer], cur.at[:, gy], bsend, brecv)
            for x in range(xs):
                cur[x, gy] = starts[gy, x]
            for copy in copies:
                copy.wait()


def per_device(nt, nx, ny, initial, source, self_block, face_blocks, coarse_block, face_code, step_counts):
    dof, xs, ys, ez = initial.shape
    assert step_counts.shape[0] == ny
    width = ys * ez
    depth = jnp.arange(ez)
    powers = (2 ** jnp.arange(6)).astype(jnp.int32)
    faces = (face_code[:, None] // powers[None, :, None, None] % 2).astype(jnp.float32)
    inside = jnp.ones((6, ez), jnp.float32).at[4].set((depth > 0) * 1.0).at[5].set((depth < ez - 1) * 1.0)
    faces = faces * inside[None, :, None, :]
    faces = jnp.pad(faces, ((0, 0), (0, 2), (0, 0), (0, 0))).reshape(xs, 8, width)

    def chunked(v):
        return v.transpose(1, 0, 2, 3).reshape(xs, dof, width)

    mine = jnp.concatenate([chunked(initial), chunked(source), faces], axis=1)
    weights = jnp.concatenate([self_block[None], face_blocks, coarse_block[None]], axis=0).reshape(8 * dof, dof)
    step = 1.0 / step_counts.astype(jnp.float32)
    gain = jnp.where(jnp.arange(MAXSTEP)[:, None] < step_counts[None, :], 0.5 * step[None, :], 0.0)
    f32, bf16 = jnp.float32, jnp.bfloat16
    tall = 2 * dof + 8
    slabs = (xs, ny, dof, width)
    dma = pltpu.SemaphoreType.DMA
    result = pl.pallas_call(
        functools.partial(kernel, nt, nx, ny),
        out_shape=jax.ShapeDtypeStruct((ny, xs, dof, width), f32),
        in_specs=[pl.BlockSpec(memory_space=pltpu.VMEM)] * 2 + [pl.BlockSpec(memory_space=pltpu.SMEM)] * 2,
        out_specs=pl.BlockSpec(memory_space=pltpu.VMEM),
        scratch_shapes=[
            pltpu.VMEM((xs, ny, tall, width), f32),
            pltpu.VMEM((8 * dof, 3 * dof), bf16),
            pltpu.VMEM((xs + 2, ny, 8 * dof, width), f32),
            pltpu.VMEM(slabs, f32),
            pltpu.VMEM(slabs, f32),
            pltpu.VMEM(slabs, f32),
            pltpu.VMEM(slabs, f32),
            pltpu.VMEM((ny, xs, dof, width), f32),
            pltpu.VMEM((ny, xs, dof, width), f32),
            pltpu.VMEM((ny + 1, xs, dof, width), f32),
            pltpu.VMEM((2, 2, ny, dof, width), f32),
            pltpu.VMEM((max(1, ITERS * (nt - 1)), xs, dof, width), f32),
            pltpu.VMEM((ny * dof, 3 * dof), bf16),
            pltpu.VMEM((dof, 6 * dof), bf16),
            dma((ny - 1,)), dma((ny - 1,)),
            dma((2, 2)), dma((2, 2)),
            dma((ny - 1,)), dma((ny - 1,)),
            dma((ny - 1,)), dma((ny - 1,)),
            dma((max(1, ITERS * (nt - 1)),)), dma((max(1, ITERS * (nt - 1)),)),
        ],
        compiler_params=pltpu.CompilerParams(collective_id=0, has_side_effects=True, vmem_limit_bytes=50 << 20),
    )(mine, weights, step, gain)
    return result.reshape(ny, xs, dof, ys, ez).transpose(0, 2, 1, 3, 4)


def solution(mesh):
    nt, nx, ny = (mesh.shape[name] for name in ("tm", "gx", "gy"))
    return jax.shard_map(
        functools.partial(per_device, nt, nx, ny),
        mesh=mesh,
        in_specs=(
            P(None, "gx", "gy", None),
            P(None, "gx", "gy", None),
            P(),
            P(),
            P(),
            P("gx", "gy", None),
            P("tm"),
        ),
        out_specs=P("tm", None, "gx", "gy", None),
        check_vma=False,
    )
```

time: 521 us -> 256 us (0.49)
  waiting for transfers between devices: 279 us -> 0 us
  Pallas kernels: 0 us -> 249 us
  matrix products: 140 us -> 0 us
  starting transfers between devices: 71.5 us -> 0 us
  local copies, waits for them, and re-layouts: 18.9 us -> 6.5 us
    ppermute x51 -> x0, waiting for transfers between devices: 279 us -> none  [the longest x24 198 us: with_halo(): lax.ppermute(tail, axis, [(i, (i + 1) % count) for i in range(count)])]
    pallas_call x0 -> x1, Pallas kernels: none -> 249 us  [per_device(): pl.pallas_call(functools.partial(kernel, nt, nx, ny), out_shape=jax.Shape...]
    dot_general x106 -> x0, matrix products: 140 us -> none  [the longest x86 131 us: batched(): return jnp.einsum('ij,sjxyz->sixyz', matrix, values, precision=HIGHEST)]
    ppermute x51 -> x0, starting transfers between devices: 71.5 us -> none  [the longest x24 47.1 us: with_halo(): lax.ppermute(head, axis, [((i + 1) % count, i) for i in range(count)])]
    slice x36 -> x0, local copies, waits for them, and re-layouts: 13 us -> none  [the longest x18 8.39 us: with_halo(): lax.slice_in_dim(cells, cells.shape[dim] - width, cells.shape[dim], axis=...]
  transfers between devices with their start and end apart: 51 -> 0, of which waited for: 42 -> 0; matrix products, arithmetic and copies ran while one was open for 18% -> 0% of each run, Pallas kernels for 0% -> 0%
where the time goes in v1:
time: 256 us
  Pallas kernels  249 us (97%)
  local copies, waits for them, and re-layouts  6.5 us (3%)
    pallas_call x1, Pallas kernels, per_device(): pl.pallas_call(functools.partial(kernel, nt, nx, ny), out_shape=jax.Shape...  249 us

profile of v1, /device:TPU:0, one launch (start us, length us, event | category | flops | bytes accessed | tf_op | source)
XLA Modules:
  0.0 256.0 jit_solution(12120663560106483158)
XLA Ops:
  0.0 0.0 copy-start.5
  0.0 0.6 copy-done.5
  0.7 0.0 copy-start.4
  0.8 0.6 copy-done.4
  1.4 0.5 fusion.2
  1.9 1.2 reshape.129
  3.1 0.0 copy-start
  3.1 0.1 copy.11
  3.1 0.9 copy-done
  4.0 0.3 reshape.130
  4.3 0.1 copy.12
  4.3 0.0 copy-start.1
  4.4 0.0 copy-start.2
  4.4 0.0 copy-start.3
  4.4 0.8 copy-done.1
  5.3 0.0 copy-done.2
  5.3 0.0 copy-done.3
  5.3 248.8 %shard_map.73 = f32[4,4,64,256]{3,2,1,0:T(8,128)S(1)} custom-call(f32[4,136,256]{2,1,0:T(8,128)S(1)} %pad_maximum_fusion.mine, f32[512,64]{1,0:T(8,128)S(1)} %bitcast.16, f32[4]{0:T(128)S(1)} %get-tuple-element.30.step_ref, f32[3,4]{1,0:T(4,128)S(1)} %fusion.4.gain_ref), custom_call_target="tpu_custom_call" | custom-call | tf_op jit(solution)/shard_map/pallas_call | solution.py:246
  254.1 0.5 reshape.128
  254.6 1.3 copy.14
  (11 shorter events, 0.2 us)
Async XLA Ops:
  0.0 0.7 copy-start.5
  0.7 0.7 copy-start.4
  3.1 1.0 copy-start
  4.3 0.9 copy-start.1
  4.4 0.9 copy-start.2
  4.4 0.9 copy-start.3

commit v2 on v1

--- a/solution.py
+++ b/solution.py
@@ -35,25 +35,40 @@
     right, left = lax.rem(gx + 1, nx), lax.rem(gx + nx - 1, nx)
     later, earlier = lax.rem(tm + 1, nt), lax.rem(tm + nt - 1, nt)
     peers = [lax.rem(gy + d, ny) for d in range(1, ny)]
+    behind = [lax.rem(gy + ny - d, ny) for d in range(1, ny)]
+    sibling = gy + 1 - 2 * lax.rem(gy, 2)
+    across = ny - 1 - gy
     xs = mine.shape[0]
     dof = weights.shape[1]
+    edges, inside = [0, xs - 1], list(range(1, xs - 1))
 
     barrier = pltpu.get_barrier_semaphore()
     for target in [{"gx": left}, {"gx": right}, {"tm": later}, {"tm": earlier}] + [{"gy": p} for p in peers]:
         pl.semaphore_signal(barrier, inc=1, device_id=target, device_id_type=MESH)
     pl.semaphore_wait(barrier, 4 + len(peers))
 
-    def exchange(source_of, target, send, receive):
-        copies = []
-        for d, peer in enumerate(peers):
-            copy = pltpu.make_async_remote_copy(
-                src_ref=source_of(peer), dst_ref=target, send_sem=send.at[d], recv_sem=receive.at[d],
-                device_id={"gy": peer}, device_id_type=MESH)
+    def remote(source, target, send, receive, device):
+        return pltpu.make_async_remote_copy(src_ref=source, dst_ref=target, send_sem=send, recv_sem=receive,
+                                            device_id=device, device_id_type=MESH)
+
+    def halo_copies(slot, y):
+        source = mid if slot == 1 else cur
+        return [
+            remote(source.at[0, y], halo.at[slot, 1, y], hsend.at[slot, 0, y], hrecv.at[slot, 1, y], {"gx": left}),
+            remote(source.at[xs - 1, y], halo.at[slot, 0, y], hsend.at[slot, 1, y], hrecv.at[slot, 0, y], {"gx": right}),
+        ]
+
+    def send_halo(slot, y):
+        for copy in halo_copies(slot, y):
             copy.start()
-            copies.append(copy)
-        return copies
-
-    copies = exchange(lambda peer: mine, field.at[:, gy], gsend, grecv)
+
+    crossing, passing, onward = {}, {}, {}
+    for x in edges + inside:
+        crossing[x] = remote(mine.at[x], field.at[x, gy], gsend.at[0, x], grecv.at[0, x], {"gy": across})
+        passing[x] = remote(mine.at[x], field.at[x, gy], gsend.at[1, x], grecv.at[1, x], {"gy": sibling})
+        onward[x] = remote(field.at[x, across], field.at[x, across], gsend.at[2, x], grecv.at[2, x], {"gy": sibling})
+        crossing[x].start()
+        passing[x].start()
 
     wide[...] = split3_weights(weights[...])
     coarse = wide[7 * dof:8 * dof, :]
@@ -71,18 +86,18 @@
 
     high, total = lax.fori_loop(0, tm * ny + gy, raise_power, (identity, jnp.zeros_like(identity)))
     mixer[...] = jnp.concatenate([split3_weights(high), split3_weights(total)], axis=1)
-    for x in range(xs):
+    for x in edges + inside:
         field[x, gy] = mine[x]
-    for copy in copies:
-        copy.wait()
-
-    def first_starts(x, _):
+        crossing[x].wait()
+        onward[x].start()
+        passing[x].wait()
+        onward[x].wait()
         for y in range(ny):
             cur[x, y] = mul(mixer[...], jnp.concatenate(
                 [split3(field[x, y, 0:dof, :]), split3(field[x, y, dof:2 * dof, :])], axis=0))
-        return 0
-
-    lax.fori_loop(0, xs, first_starts, 0)
+        if x == edges[-1]:
+            for y in range(ny):
+                send_halo(0, y)
 
     step = step_ref[gy]
 
@@ -109,17 +124,8 @@
         total = total + mask(4) * below
         return total + mask(5) * above
 
-    def stage(second, finish):
-        source = mid if second else cur
-        slot = 1 if second else 0
-        to_left = pltpu.make_async_remote_copy(
-            src_ref=source.at[0], dst_ref=halo.at[slot, 1], send_sem=hsend.at[slot, 0], recv_sem=hrecv.at[slot, 1],
-            device_id={"gx": left}, device_id_type=MESH)
-        to_right = pltpu.make_async_remote_copy(
-            src_ref=source.at[xs - 1], dst_ref=halo.at[slot, 0], send_sem=hsend.at[slot, 1], recv_sem=hrecv.at[slot, 0],
-            device_id={"gx": right}, device_id_type=MESH)
-        to_left.start()
-        to_right.start()
+    def stage(slot, finish, after_inside, after_edge):
+        source = mid if slot == 1 else cur
 
         def products(x, _):
             for y in range(ny):
@@ -134,75 +140,92 @@
             return 0
 
         lax.fori_loop(1, xs - 1, inner, 0)
-        to_left.wait()
-        to_right.wait()
+        after_inside()
         for y in range(ny):
+            for copy in halo_copies(slot, y):
+                copy.wait()
             prod[0, y, dof:2 * dof, :] = mul(wide[dof:2 * dof, :], split3(halo[slot, 0, y]))
             prod[xs + 1, y, 2 * dof:3 * dof, :] = mul(wide[2 * dof:3 * dof, :], split3(halo[slot, 1, y]))
-        for x in (0, xs - 1):
-            for y in range(ny):
+            for x in edges:
                 finish(x, y, combine(x, y))
+            after_edge(y)
+
+    def nothing(*_):
+        return None
+
+    def to_middle(x, y, rate):
+        slope[x, y] = rate
+        mid[x, y] = cur[x, y] + step * rate
 
     def advance(number, _):
         gain = gain_ref[number, gy]
 
-        def to_middle(x, y, rate):
-            slope[x, y] = rate
-            mid[x, y] = cur[x, y] + step * rate
-
         def to_next(x, y, rate):
             cur[x, y] = cur[x, y] + gain * (slope[x, y] + rate)
 
-        stage(False, to_middle)
-        stage(True, to_next)
+        stage(0, to_middle, nothing, functools.partial(send_halo, 1))
+        stage(1, to_next, nothing, functools.partial(send_halo, 0))
         return 0
 
+    def incoming(at, x):
+        return jnp.where(tm == 0, mine[x, 0:dof, :], arrived[at, x])
+
     for iteration in range(ITERS):
+        last = iteration == ITERS - 1
+
         def keep_coarse(x, _):
             for y in range(ny):
                 corr[x, y] = mul(coarse, split3(cur[x, y]))
             return 0
 
         lax.fori_loop(0, xs, keep_coarse, 0)
-        lax.fori_loop(0, MAXSTEP, advance, 0)
-
-        def correct(x, _):
-            for y in range(ny):
-                corr[x, y] = cur[x, y] - corr[x, y]
-            return 0
-
-        lax.fori_loop(0, xs, correct, 0)
-        copies = exchange(lambda peer: corr.at[:, peer], recv.at[gy], asend, arecv)
-        for x in range(xs):
+        lax.fori_loop(0, MAXSTEP - 1, advance, 0)
+        gain = gain_ref[MAXSTEP - 1, gy]
+        giving = {}
+
+        def to_correction(x, y, rate):
+            corr[x, y] = cur[x, y] + gain * (slope[x, y] + rate) - corr[x, y]
+
+        def give(places):
+            for x in places:
+                for d, peer in enumerate(peers):
+                    giving[x, d] = remote(corr.at[x, peer], recv.at[gy, x], asend.at[x, d], arecv.at[x, d], {"gy": peer})
+                    giving[x, d].start()
+
+        stage(0, to_middle, nothing, functools.partial(send_halo, 1))
+        stage(1, to_correction, functools.partial(give, inside), nothing)
+        give(edges)
+
+        relays = {}
+
+        def relay(number, x, entering):
+            at = iteration * (nt - 1) + number
+            starts[ny, x] = mul(powers[(ny - 1) * dof:, :], split3(entering)) + local[ny - 1, x]
+            relays[x] = remote(starts.at[ny, x], arrived.at[at, x], tsend.at[at, x], trecv.at[at, x], {"tm": later})
+            relays[x].start()
+
+        for x in inside + edges:
             recv[gy, x] = corr[x, gy]
-        for copy in copies:
-            copy.wait()
-
-        def run_local(x, _):
+            for d in range(len(peers)):
+                giving[x, d].wait()
             now = recv[0, x]
             local[0, x] = now
             for j in range(1, ny):
                 now = mul(coarse, split3(now)) + recv[j, x]
                 local[j, x] = now
-            return 0
-
-        lax.fori_loop(0, xs, run_local, 0)
-        for x in range(xs):
-            starts[0, x] = mine[x, 0:dof, :]
-        for relay in range(nt - 1):
-            at = iteration * (nt - 1) + relay
-            for x in range(xs):
-                starts[ny, x] = mul(powers[(ny - 1) * dof:, :], split3(starts[0, x])) + local[ny - 1, x]
-            copy = pltpu.make_async_remote_copy(
-                src_ref=starts.at[ny], dst_ref=arrived.at[at], send_sem=tsend.at[at], recv_sem=trecv.at[at],
-                device_id={"tm": later}, device_id_type=MESH)
-            copy.start()
-            copy.wait()
-            for x in range(xs):
-                starts[0, x] = jnp.where(tm == 0, mine[x, 0:dof, :], arrived[at, x])
-        last = iteration == ITERS - 1
-
-        def finish_all(x, _):
+            if nt > 1:
+                relay(0, x, mine[x, 0:dof, :])
+        for number in range(1, nt - 1):
+            for x in inside + edges:
+                relays[x].wait()
+                relay(number, x, incoming(iteration * (nt - 1) + number - 1, x))
+        taking = {}
+        for x in inside + edges:
+            if nt > 1:
+                relays[x].wait()
+                starts[0, x] = incoming(iteration * (nt - 1) + nt - 2, x)
+            else:
+                starts[0, x] = mine[x, 0:dof, :]
             shares = mul(powers[...], split3(starts[0, x]))
             for j in range(ny):
                 ended = shares[j * dof:(j + 1) * dof, :] + local[j, x]
@@ -210,20 +233,25 @@
                     out[j, x] = ended
                 elif j < ny - 1:
                     starts[j + 1, x] = ended
-            return 0
-
-        lax.fori_loop(0, xs, finish_all, 0)
+            if not last:
+                cur[x, gy] = starts[gy, x]
+                for d, peer in enumerate(peers):
+                    taking[x, d] = remote(starts.at[peer, x], cur.at[x, gy], bsend.at[x, d], brecv.at[x, d], {"gy": peer})
+                    taking[x, d].start()
         if not last:
-            copies = exchange(lambda peer: starts.at[peer], cur.at[:, gy], bsend, brecv)
-            for x in range(xs):
-                cur[x, gy] = starts[gy, x]
-            for copy in copies:
-                copy.wait()
+            send_halo(0, gy)
+            for d in range(len(peers)):
+                for x in edges:
+                    taking[x, d].wait()
+                send_halo(0, behind[d])
+            for x in inside:
+                for d in range(len(peers)):
+                    taking[x, d].wait()
 
 
 def per_device(nt, nx, ny, initial, source, self_block, face_blocks, coarse_block, face_code, step_counts):
     dof, xs, ys, ez = initial.shape
-    assert step_counts.shape[0] == ny
+    assert step_counts.shape[0] == ny == 4
     width = ys * ez
     depth = jnp.arange(ez)
     powers = (2 ** jnp.arange(6)).astype(jnp.int32)
@@ -263,11 +291,11 @@
             pltpu.VMEM((max(1, ITERS * (nt - 1)), xs, dof, width), f32),
             pltpu.VMEM((ny * dof, 3 * dof), bf16),
             pltpu.VMEM((dof, 6 * dof), bf16),
-            dma((ny - 1,)), dma((ny - 1,)),
-            dma((2, 2)), dma((2, 2)),
-            dma((ny - 1,)), dma((ny - 1,)),
-            dma((ny - 1,)), dma((ny - 1,)),
-            dma((max(1, ITERS * (nt - 1)),)), dma((max(1, ITERS * (nt - 1)),)),
+            dma((3, xs)), dma((3, xs)),
+            dma((2, 2, ny)), dma((2, 2, ny)),
+            dma((xs, ny - 1)), dma((xs, ny - 1)),
+            dma((xs, ny - 1)), dma((xs, ny - 1)),
+            dma((max(1, ITERS * (nt - 1)), xs)), dma((max(1, ITERS * (nt - 1)), xs)),
         ],
         compiler_params=pltpu.CompilerParams(collective_id=0, has_side_effects=True, vmem_limit_bytes=50 << 20),
     )(mine, weights, step, gain)

time: 256 us -> 192 us (0.75)
  Pallas kernels: 249 us -> 185 us
    pallas_call x1, Pallas kernels: 249 us -> 185 us  [per_device(): pl.pallas_call(functools.partial(kernel, nt, nx, ny), out_shape=jax.Shape...]
where the time goes in v2:
time: 192 us
  Pallas kernels  185 us (96%)
  local copies, waits for them, and re-layouts  6.5 us (3%)
    pallas_call x1, Pallas kernels, per_device(): pl.pallas_call(functools.partial(kernel, nt, nx, ny), out_shape=jax.Shape...  185 us

profile of v2, /device:TPU:0, one launch (start us, length us, event | category | flops | bytes accessed | tf_op | source)
XLA Modules:
  0.0 192.2 jit_solution(13111736666391086579)
XLA Ops:
  0.0 0.0 copy-start.5
  0.0 0.6 copy-done.5
  0.7 0.0 copy-start.4
  0.8 0.6 copy-done.4
  1.4 0.5 fusion.2
  1.9 1.2 reshape.129
  3.1 0.0 copy-start
  3.1 0.1 copy.11
  3.1 0.9 copy-done
  4.0 0.3 reshape.130
  4.3 0.1 copy.12
  4.3 0.0 copy-start.1
  4.4 0.0 copy-start.2
  4.4 0.0 copy-start.3
  4.4 0.8 copy-done.1
  5.3 0.0 copy-done.2
  5.3 0.0 copy-done.3
  5.3 185.0 %shard_map.73 = f32[4,4,64,256]{3,2,1,0:T(8,128)S(1)} custom-call(f32[4,136,256]{2,1,0:T(8,128)S(1)} %pad_maximum_fusion.mine, f32[512,64]{1,0:T(8,128)S(1)} %bitcast.16, f32[4]{0:T(128)S(1)} %get-tuple-element.30.step_ref, f32[3,4]{1,0:T(4,128)S(1)} %fusion.4.gain_ref), custom_call_target="tpu_custom_call" | custom-call | tf_op jit(solution)/shard_map/pallas_call | solution.py:274
  190.3 0.5 reshape.128
  190.9 1.3 copy.14
  (11 shorter events, 0.2 us)
Async XLA Ops:
  0.0 0.7 copy-start.5
  0.7 0.7 copy-start.4
  3.1 1.0 copy-start
  4.3 0.9 copy-start.1
  4.4 0.9 copy-start.2
  4.4 0.9 copy-start.3

commit v3 on v2

--- a/solution.py
+++ b/solution.py
@@ -34,10 +34,9 @@
     tm, gx, gy = lax.axis_index("tm"), lax.axis_index("gx"), lax.axis_index("gy")
     right, left = lax.rem(gx + 1, nx), lax.rem(gx + nx - 1, nx)
     later, earlier = lax.rem(tm + 1, nt), lax.rem(tm + nt - 1, nt)
-    peers = [lax.rem(gy + d, ny) for d in range(1, ny)]
-    behind = [lax.rem(gy + ny - d, ny) for d in range(1, ny)]
     sibling = gy + 1 - 2 * lax.rem(gy, 2)
-    across = ny - 1 - gy
+    across, beyond = ny - 1 - gy, ny - 1 - sibling
+    peers = [across, beyond, sibling]
     xs = mine.shape[0]
     dof = weights.shape[1]
     edges, inside = [0, xs - 1], list(range(1, xs - 1))
@@ -96,7 +95,7 @@
             cur[x, y] = mul(mixer[...], jnp.concatenate(
                 [split3(field[x, y, 0:dof, :]), split3(field[x, y, dof:2 * dof, :])], axis=0))
         if x == edges[-1]:
-            for y in range(ny):
+            for y in peers + [gy]:
                 send_halo(0, y)
 
     step = step_ref[gy]
@@ -107,7 +106,7 @@
         def mask(f):
             return field[x, y, 2 * dof + f:2 * dof + f + 1, :]
 
-        lower, upper = prod.at[x + 1, (y + ny - 1) % ny], prod.at[x + 1, (y + 1) % ny]
+        lower, upper = prod.at[x + 1, lax.rem(y + ny - 1, ny)], prod.at[x + 1, lax.rem(y + 1, ny)]
 
         def face(f):
             return slice((f + 1) * dof, (f + 2) * dof)
@@ -141,7 +140,7 @@
 
         lax.fori_loop(1, xs - 1, inner, 0)
         after_inside()
-        for y in range(ny):
+        for y in peers + [gy]:
             for copy in halo_copies(slot, y):
                 copy.wait()
             prod[0, y, dof:2 * dof, :] = mul(wide[dof:2 * dof, :], split3(halo[slot, 0, y]))
@@ -186,15 +185,21 @@
         def to_correction(x, y, rate):
             corr[x, y] = cur[x, y] + gain * (slope[x, y] + rate) - corr[x, y]
 
-        def give(places):
+        for x in range(xs):
+            for d, peer in enumerate(peers):
+                giving[x, d] = remote(corr.at[x, peer], recv.at[gy, x], asend.at[x, d], arecv.at[x, d], {"gy": peer})
+
+        def give(places, reached):
             for x in places:
                 for d, peer in enumerate(peers):
-                    giving[x, d] = remote(corr.at[x, peer], recv.at[gy, x], asend.at[x, d], arecv.at[x, d], {"gy": peer})
-                    giving[x, d].start()
+                    if any(peer is y for y in reached):
+                        giving[x, d].start()
+
+        def give_edge(y):
+            give(edges, [y])
 
         stage(0, to_middle, nothing, functools.partial(send_halo, 1))
-        stage(1, to_correction, functools.partial(give, inside), nothing)
-        give(edges)
+        stage(1, to_correction, functools.partial(give, inside, peers), give_edge)
 
         relays = {}
 
@@ -204,7 +209,9 @@
             relays[x] = remote(starts.at[ny, x], arrived.at[at, x], tsend.at[at, x], trecv.at[at, x], {"tm": later})
             relays[x].start()
 
-        for x in inside + edges:
+        taking = {}
+
+        def sweep_from_zero(x):
             recv[gy, x] = corr[x, gy]
             for d in range(len(peers)):
                 giving[x, d].wait()
@@ -215,12 +222,8 @@
                 local[j, x] = now
             if nt > 1:
                 relay(0, x, mine[x, 0:dof, :])
-        for number in range(1, nt - 1):
-            for x in inside + edges:
-                relays[x].wait()
-                relay(number, x, incoming(iteration * (nt - 1) + number - 1, x))
-        taking = {}
-        for x in inside + edges:
+
+        def sweep_on(x):
             if nt > 1:
                 relays[x].wait()
                 starts[0, x] = incoming(iteration * (nt - 1) + nt - 2, x)
@@ -238,12 +241,22 @@
                 for d, peer in enumerate(peers):
                     taking[x, d] = remote(starts.at[peer, x], cur.at[x, gy], bsend.at[x, d], brecv.at[x, d], {"gy": peer})
                     taking[x, d].start()
+
+        for places in (inside, edges):
+            for x in places:
+                sweep_from_zero(x)
+            for number in range(1, nt - 1):
+                for x in places:
+                    relays[x].wait()
+                    relay(number, x, incoming(iteration * (nt - 1) + number - 1, x))
+            for x in places:
+                sweep_on(x)
         if not last:
             send_halo(0, gy)
             for d in range(len(peers)):
                 for x in edges:
                     taking[x, d].wait()
-                send_halo(0, behind[d])
+                send_halo(0, peers[d])
             for x in inside:
                 for d in range(len(peers)):
                     taking[x, d].wait()

time: 192 us -> 186 us (0.969)
  Pallas kernels: 185 us -> 179 us
    pallas_call x1, Pallas kernels: 185 us -> 179 us  [per_device(): pl.pallas_call(functools.partial(kernel, nt, nx, ny), out_shape=jax.Shape...]
where the time goes in v3:
time: 186 us
  Pallas kernels  179 us (96%)
  local copies, waits for them, and re-layouts  6.5 us (3%)
    pallas_call x1, Pallas kernels, per_device(): pl.pallas_call(functools.partial(kernel, nt, nx, ny), out_shape=jax.Shape...  179 us

profile of v3, /device:TPU:0, one launch (start us, length us, event | category | flops | bytes accessed | tf_op | source)
XLA Modules:
  0.0 186.2 jit_solution(10262814784907116193)
XLA Ops:
  0.0 0.0 copy-start.5
  0.0 0.6 copy-done.5
  0.7 0.0 copy-start.4
  0.8 0.6 copy-done.4
  1.4 0.5 fusion.2
  1.9 1.2 reshape.129
  3.1 0.0 copy-start
  3.1 0.1 copy.11
  3.1 0.9 copy-done
  4.0 0.3 reshape.130
  4.3 0.1 copy.12
  4.3 0.0 copy-start.1
  4.4 0.0 copy-start.2
  4.4 0.0 copy-start.3
  4.4 0.8 copy-done.1
  5.3 0.0 copy-done.2
  5.3 0.0 copy-done.3
  5.3 179.0 %shard_map.73 = f32[4,4,64,256]{3,2,1,0:T(8,128)S(1)} custom-call(f32[4,136,256]{2,1,0:T(8,128)S(1)} %pad_maximum_fusion.mine, f32[512,64]{1,0:T(8,128)S(1)} %bitcast.16, f32[4]{0:T(128)S(1)} %get-tuple-element.30.step_ref, f32[3,4]{1,0:T(4,128)S(1)} %fusion.4.gain_ref), custom_call_target="tpu_custom_call" | custom-call | tf_op jit(solution)/shard_map/pallas_call | solution.py:287
  184.3 0.5 reshape.128
  184.8 1.3 copy.14
  (11 shorter events, 0.2 us)
Async XLA Ops:
  0.0 0.7 copy-start.5
  0.7 0.7 copy-start.4
  3.1 1.0 copy-start
  4.3 0.9 copy-start.1
  4.4 0.9 copy-start.2
  4.4 0.9 copy-start.3
